TPU v7x, 32 devices: a whole 2x2x4 slice. The times are simulated.
32 devices in a mesh: dp: 8 (over y, x, core), seq: 4 (over z).
Axes of the slice: x: 2, y: 2, z: 4, core: 2. Of those that a mesh axis runs over, the one named last changes fastest.
Arguments:
- inputs: bfloat16 [32, 512, 1024], P('dp', 'seq'), may hold values from -6 to 6
- cotangent: bfloat16 [32, 512, 1024], P('dp', 'seq'), may hold values from -6 to 6
- lengths: int32 [32], P('dp'), may hold values from 80 to 512, as said below
- w_query: bfloat16 [1024, 1024], replicated, may hold values from -0.1875 to 0.1875
- b_query: float32 [1024], replicated, may hold values from -4 to 4
- w_key: bfloat16 [1024, 1024], replicated, may hold values from -0.1875 to 0.1875
- w_value: bfloat16 [1024, 1024], replicated, may hold values from -0.1875 to 0.1875
- b_value: float32 [1024], replicated, may hold values from -4 to 4
- w_output: bfloat16 [1024, 1024], replicated, may hold values from -0.75 to 0.75
- b_output: float32 [1024], replicated, may hold values from -4 to 4
- gain_first: float32 [1024], replicated, may hold values from 0.5 to 1.5
- shift_first: float32 [1024], replicated, may hold values from -4 to 4
- w_in: bfloat16 [1024, 4096], replicated, may hold values from -0.1875 to 0.1875
- b_in: float32 [4096], replicated, may hold values from -4 to 4
- w_out: bfloat16 [4096, 1024], replicated, may hold values from -0.1875 to 0.1875
- b_out: float32 [1024], replicated, may hold values from -4 to 4
- gain_second: float32 [1024], replicated, may hold values from 0.5 to 1.5
- shift_second: float32 [1024], replicated, may hold values from -4 to 4
Outputs:
- outputs: bfloat16 [32, 512, 1024], P('dp', 'seq')
- grad_inputs: float32 [32, 512, 1024], P('dp', 'seq')
- grad_w_query: float32 [1024, 1024], P(('dp', 'seq'))
- grad_b_query: float32 [1024], P(('dp', 'seq'))
- grad_w_key: float32 [1024, 1024], P(('dp', 'seq'))
- grad_w_value: float32 [1024, 1024], P(('dp', 'seq'))
- grad_b_value: float32 [1024], P(('dp', 'seq'))
- grad_w_output: float32 [1024, 1024], P(('dp', 'seq'))
- grad_b_output: float32 [1024], P(('dp', 'seq'))
- grad_gain_first: float32 [1024], P(('dp', 'seq'))
- grad_shift_first: float32 [1024], P(('dp', 'seq'))
- grad_w_in: float32 [1024, 4096], P(('dp', 'seq'))
- grad_b_in: float32 [4096], P(('dp', 'seq'))
- grad_w_out: float32 [4096, 1024], P(('dp', 'seq'))
- grad_b_out: float32 [1024], P(('dp', 'seq'))
- grad_gain_second: float32 [1024], P(('dp', 'seq'))
- grad_shift_second: float32 [1024], P(('dp', 'seq'))
Inputs may be any that keep to these rules, and one draw needn't show every extreme that they name: A page's real tokens are its first lengths slots. Some page is full and some page has exactly 80 real tokens.
All inputs are finite; a program needn't handle non-finite values.
Results may differ from a plain program's by a relative error of at most 0.015.
Values may be sent and summed in bfloat16 or wider, within the bound.
No kernel may reach another device: no remote copies, remote signals or barrier semaphores. Data moves between devices by JAX's collectives and lax.ppermute only.
A program may use at most 320 MiB of HBM per device.

v0:
```python
import math
import jax
import jax.numpy as jnp
from jax import lax
from jax.sharding import PartitionSpec as P

HEAD_DIM = 64
MICRO = 4
EPS = 1e-05


def dense(left, right):
    return jnp.dot(left, right, preferred_element_type=jnp.float32)


def dense_back(left, right):
    return lax.dot_general(
        left, right, (((1,), (1,)), ((), ())), preferred_element_type=jnp.float32
    )


def weight_term(left, right):
    return lax.dot_general(
        left, right, (((0,), (0,)), ((), ())), preferred_element_type=jnp.float32
    )


def norm_parts(summed):
    centred = summed - jnp.mean(summed, -1, keepdims=True)
    factor = lax.rsqrt(jnp.mean(centred * centred, -1, keepdims=True) + EPS)
    return (centred * factor, factor)


def norm_back(grad_normed, normed, factor):
    return factor * (
        grad_normed
        - jnp.mean(grad_normed, -1, keepdims=True)
        - normed * jnp.mean(grad_normed * normed, -1, keepdims=True)
    )


def gelu_slope(inner):
    cumulative = 0.5 * (1.0 + lax.erf(inner * 0.7071067811865476))
    density = jnp.exp(-0.5 * inner * inner) * 0.3989422804014327
    return cumulative + inner * density


def add_pairs(left, right):
    return tuple((first + second for first, second in zip(left, right)))


def on_device(
    inputs,
    cotangent,
    lengths,
    w_query,
    b_query,
    w_key,
    w_value,
    b_value,
    w_output,
    b_output,
    gain_first,
    shift_first,
    w_in,
    b_in,
    w_out,
    b_out,
    gain_second,
    shift_second,
):
    pages_dev, slots_dev, width = inputs.shape
    seq_count = lax.axis_size("seq")
    slots_all = slots_dev * seq_count
    head_size = HEAD_DIM
    local_width = width // seq_count
    heads_dev = local_width // head_size
    scale = 1.0 / math.sqrt(head_size)
    group = pages_dev // MICRO
    rows = group * slots_dev
    first_slot = lax.axis_index("seq") * slots_dev
    key_place = jnp.arange(slots_all, dtype=jnp.int32)
    row_place = first_slot + jnp.arange(slots_dev, dtype=jnp.int32)
    lower_shapes = (w_query.shape, b_query.shape, w_key.shape, w_value.shape, b_value.shape)
    upper_shapes = (
        w_output.shape,
        b_output.shape,
        gain_first.shape,
        shift_first.shape,
        w_in.shape,
        b_in.shape,
        w_out.shape,
        b_out.shape,
        gain_second.shape,
        shift_second.shape,
    )
    lower_totals = tuple((jnp.zeros(shape, jnp.float32) for shape in lower_shapes))
    upper_totals = tuple((jnp.zeros(shape, jnp.float32) for shape in upper_shapes))
    results = []
    input_grads = []
    for micro_step in range(MICRO):
        block = inputs[micro_step * group : (micro_step + 1) * group].reshape(rows, width)
        block_lengths = lengths[micro_step * group : (micro_step + 1) * group]
        queries = (dense(block, w_query) + b_query).astype(jnp.bfloat16)
        keys_local = dense(block, w_key).astype(jnp.bfloat16)
        values = (dense(block, w_value) + b_value).astype(jnp.bfloat16)
        packed = jnp.stack([queries, keys_local, values]).reshape(
            3, group, slots_dev, seq_count, local_width
        )
        spread = lax.all_to_all(packed, "seq", split_axis=3, concat_axis=2, tiled=True)
        head_q = spread[0].reshape(group, slots_all, heads_dev, head_size)
        head_k = spread[1].reshape(group, slots_all, heads_dev, head_size)
        head_v = spread[2].reshape(group, slots_all, heads_dev, head_size)
        key_live = key_place[None, :] < block_lengths[:, None]
        scores = (
            jnp.einsum("gqhd,gkhd->ghqk", head_q, head_k, preferred_element_type=jnp.float32)
            * scale
        )
        scores = jnp.where(key_live[:, None, None, :], scores, -1e30)
        largest = jnp.max(scores, -1, keepdims=True)
        expon = jnp.exp(scores - largest)
        totals_row = jnp.sum(expon, -1, keepdims=True)
        probs = expon / totals_row
        log_total = largest + jnp.log(totals_row)
        context = jnp.einsum(
            "ghqk,gkhd->gqhd",
            probs.astype(jnp.bfloat16),
            head_v,
            preferred_element_type=jnp.float32,
        ).astype(jnp.bfloat16)
        context = context.reshape(group, slots_all, 1, local_width)
        gathered = lax.all_to_all(context, "seq", split_axis=1, concat_axis=2, tiled=True).reshape(
            rows, width
        )
        attended = dense(gathered, w_output) + b_output
        normed_first, factor_first = norm_parts(block.astype(jnp.float32) + attended)
        hidden = normed_first * gain_first + shift_first
        hidden_low = hidden.astype(jnp.bfloat16)
        inner = dense(hidden_low, w_in) + b_in
        activated = jax.nn.gelu(inner, approximate=False).astype(jnp.bfloat16)
        branch = dense(activated, w_out) + b_out
        normed_second, factor_second = norm_parts(hidden + branch)
        result = normed_second * gain_second + shift_second
        results.append(result.astype(jnp.bfloat16).reshape(group, slots_dev, width))
        row_live = (
            (row_place[None, :] < block_lengths[:, None]).astype(jnp.float32).reshape(rows, 1)
        )
        upstream = (
            cotangent[micro_step * group : (micro_step + 1) * group]
            .reshape(rows, width)
            .astype(jnp.float32)
            * row_live
        )
        g_gain_second = jnp.sum(upstream * normed_second, 0)
        g_shift_second = jnp.sum(upstream, 0)
        d_second = norm_back(upstream * gain_second, normed_second, factor_second)
        d_branch = d_second.astype(jnp.bfloat16)
        g_w_out = weight_term(activated, d_branch)
        g_b_out = jnp.sum(d_branch.astype(jnp.float32), 0)
        d_inner = (dense_back(d_branch, w_out) * gelu_slope(inner)).astype(jnp.bfloat16)
        g_w_in = weight_term(hidden_low, d_inner)
        g_b_in = jnp.sum(d_inner.astype(jnp.float32), 0)
        d_hidden = d_second + dense_back(d_inner, w_in)
        g_gain_first = jnp.sum(d_hidden * normed_first, 0)
        g_shift_first = jnp.sum(d_hidden, 0)
        d_first = norm_back(d_hidden * gain_first, normed_first, factor_first)
        d_attended = d_first.astype(jnp.bfloat16)
        g_w_output = weight_term(gathered, d_attended)
        g_b_output = jnp.sum(d_attended.astype(jnp.float32), 0)
        upper_terms = (
            g_w_output,
            g_b_output,
            g_gain_first,
            g_shift_first,
            g_w_in,
            g_b_in,
            g_w_out,
            g_b_out,
            g_gain_second,
            g_shift_second,
        )
        d_context = dense_back(d_attended, w_output).astype(jnp.bfloat16)
        d_context = d_context.reshape(group, slots_dev, seq_count, local_width)
        head_grad = lax.all_to_all(d_context, "seq", split_axis=2, concat_axis=1, tiled=True)
        head_grad = head_grad.reshape(group, slots_all, heads_dev, head_size)
        scores_again = (
            jnp.einsum("gqhd,gkhd->ghqk", head_q, head_k, preferred_element_type=jnp.float32)
            * scale
        )
        scores_again = jnp.where(key_live[:, None, None, :], scores_again, -1e30)
        probs_again = jnp.exp(scores_again - log_total)
        d_probs = jnp.einsum(
            "gqhd,gkhd->ghqk", head_grad, head_v, preferred_element_type=jnp.float32
        )
        d_vals = jnp.einsum(
            "ghqk,gqhd->gkhd",
            probs_again.astype(jnp.bfloat16),
            head_grad,
            preferred_element_type=jnp.float32,
        )
        inner_sum = jnp.sum(probs_again * d_probs, -1, keepdims=True)
        d_scores = (probs_again * (d_probs - inner_sum)).astype(jnp.bfloat16)
        d_queries = (
            jnp.einsum("ghqk,gkhd->gqhd", d_scores, head_k, preferred_element_type=jnp.float32)
            * scale
        )
        d_keys = (
            jnp.einsum("ghqk,gqhd->gkhd", d_scores, head_q, preferred_element_type=jnp.float32)
            * scale
        )
        stacked = jnp.stack([d_queries, d_keys, d_vals]).astype(jnp.bfloat16)
        stacked = stacked.reshape(3, group, slots_all, 1, local_width)
        returned = lax.all_to_all(stacked, "seq", split_axis=2, concat_axis=3, tiled=True).reshape(
            3, rows, width
        )
        g_w_query = weight_term(block, returned[0])
        g_b_query = jnp.sum(returned[0].astype(jnp.float32), 0)
        g_w_key = weight_term(block, returned[1])
        g_w_value = weight_term(block, returned[2])
        g_b_value = jnp.sum(returned[2].astype(jnp.float32), 0)
        grad_block = (
            d_first
            + dense_back(returned[0], w_query)
            + dense_back(returned[1], w_key)
            + dense_back(returned[2], w_value)
        )
        input_grads.append(grad_block.reshape(group, slots_dev, width))
        lower_terms = (g_w_query, g_b_query, g_w_key, g_w_value, g_b_value)
        lower_totals = add_pairs(lower_totals, lower_terms)
        upper_totals = add_pairs(upper_totals, upper_terms)
    summed = lax.psum_scatter(
        lower_totals + upper_totals, ("dp", "seq"), scatter_dimension=0, tiled=True
    )
    lower_totals = tuple(summed[:5])
    upper_totals = tuple(summed[5:])
    return (
        jnp.concatenate(results, 0),
        jnp.concatenate(input_grads, 0),
        lower_totals[0],
        lower_totals[1],
        lower_totals[2],
        lower_totals[3],
        lower_totals[4],
        upper_totals[0],
        upper_totals[1],
        upper_totals[2],
        upper_totals[3],
        upper_totals[4],
        upper_totals[5],
        upper_totals[6],
        upper_totals[7],
        upper_totals[8],
        upper_totals[9],
    )


def solution(mesh):
    in_specs = (
        P("dp", "seq", None),
        P("dp", "seq", None),
        P("dp"),
        P(),
        P(),
        P(),
        P(),
        P(),
        P(),
        P(),
        P(),
        P(),
        P(),
        P(),
        P(),
        P(),
        P(),
        P(),
    )
    out_specs = (
        P("dp", "seq", None),
        P("dp", "seq", None),
        P(("dp", "seq"), None),
        P(("dp", "seq")),
        P(("dp", "seq"), None),
        P(("dp", "seq"), None),
        P(("dp", "seq")),
        P(("dp", "seq"), None),
        P(("dp", "seq")),
        P(("dp", "seq")),
        P(("dp", "seq")),
        P(("dp", "seq"), None),
        P(("dp", "seq")),
        P(("dp", "seq"), None),
        P(("dp", "seq")),
        P(("dp", "seq")),
        P(("dp", "seq")),
    )
    return jax.shard_map(
        on_device, mesh=mesh, in_specs=in_specs, out_specs=out_specs, check_vma=False
    )
```

profile of v0, /device:TPU:0, one launch (start us, length us, event | category | flops | bytes accessed | tf_op | source)
XLA Modules:
  0.0 1803.7 jit_solution(12697095188819701354)
XLA Ops:
  22.5 6.3 all-to-all-start.6
  44.0 5.1 all-to-all-done.6
  96.9 4.7 all-to-all-start
  168.9 5.2 all-to-all-start.1
  211.2 5.3 all-to-all-start.3
  222.2 5.4 convolution_add_fusion.3
  227.7 6.3 fusion.292
  234.0 5.5 all-to-all-start.5
  245.2 5.4 convolution_add_fusion.2
  250.7 5.6 fusion.289
  257.9 5.3 all-to-all-start.7
  268.8 4.7 convolution_add_fusion.1
  273.6 9.7 fusion.298
  288.9 4.7 convolution_add_fusion
  293.7 9.1 fusion.295
  307.5 7.4 convert_reduce_fusion.3
  315.0 7.5 convert_reduce_fusion
  323.3 8.1 convert_reduce_fusion.1
  334.3 7.5 convert_reduce_fusion.2
  377.8 5.1 all-to-all-start.8
  382.9 7.4 add_add_fusion.2
  390.4 5.2 all-to-all-start.12
  395.9 5.2 multiply_reduce_fusion.3
  410.3 4.8 multiply_convert_fusion.3
  431.0 5.4 all-to-all-start.10
  466.4 27.6 %all-to-all-done.9 = bf16[3,1,512,1,256]{4,0,3,1,2:T(4,128)(2,1)} async-done(((bf16[3,1,512,1,256]{4,0,3,1,2:T(4,128)(2,1)}), bf16[3,1,512,1,256]{4,0,3,1,2:T(4,128)(2,1)}, u32[]{:S(2)}, u32[]{:S(2)}) %all-to-all-start.9) | async-done | bytes 786464 | tf_op jit(solution)/shard_map/all_to_all | solution.py:213
  494.0 4.7 all-to-all-start.13
  517.2 5.0 multiply_reduce_fusion.2
  522.2 16.7 all-to-all-done.13
  543.2 4.7 multiply_convert_fusion.2
  557.7 17.1 all-to-all-done.15
  587.9 16.9 all-to-all-done.11
  613.1 5.4 copy.279
  625.0 5.4 copy.277
  636.9 5.4 copy.275
  644.0 9.7 fusion.252
  653.7 9.8 fusion.246
  663.5 9.7 fusion.240
  673.2 24.1 %add_add_fusion = f32[4096,1024]{1,0:T(8,128)} fusion(f32[4096,1024]{1,0:T(8,128)} %fusion.240, f32[4096,1024]{1,0:T(8,128)} %fusion.252, f32[4096,1024]{1,0:T(8,128)} %fusion.246, f32[128,1024]{1,0:T(8,128)S(1)} %copy-done.40, f32[128,4096]{1,0:T(8,128)S(1)} %copy-done.25), kind=kOutput, calls=%fused_computation | convolution fusion | flops 1120534528 | bytes 69730304 | tf_op jit(solution)/shard_map/dot_general | solution.py:23
  698.4 9.4 fusion.257
  707.9 8.2 fusion.260
  716.1 8.2 fusion.263
  724.3 23.2 %add_add_fusion.1 = f32[1024,4096]{1,0:T(8,128)} fusion(f32[1024,4096]{1,0:T(8,128)} %fusion.257, f32[1024,4096]{1,0:T(8,128)} %fusion.263, f32[1024,4096]{1,0:T(8,128)} %fusion.260, bf16[128,4096]{1,0:T(8,128)(2,1)S(1)} %copy-done.49, f32[128,1024]{1,0:T(8,128)S(1)} %copy-done.14, f32[128]{0:T(128)S(1)} %copy-done.181, f32[128]{0:T(128)S(1)} %copy-done.149, ...), kind=kOutput, calls=%fused_computation.1 | convolution fusion | flops 1086980096 | bytes 68690944 | tf_op jit(solution)/shard_map/dot_general | solution.py:23
  756.1 39.9 %all-reduce.9 = (f32[1024]{0:T(1024)S(1)}, f32[1024]{0:T(1024)S(1)}, f32[1024]{0:T(1024)S(1)}, f32[1024]{0:T(1024)S(1)}, f32[1024]{0:T(1024)S(1)}, /*index=5*/f3...) all-reduce(f32[1024]{0:T(1024)S(1)} %bitcast.508, ...), channel_id=3, replica_groups=mesh['dp'=8,'seq'=4] {'dp','seq'}, use_global_device_ids=true, to_apply=%region_49.50.clone | all-reduce | flops 12288 | bytes 98304
  816.2 101.8 %reduce-scatter.21.cloned.1.call-done = f32[32,1024]{1,0:T(8,128)} async-done(((f32[1024,1024]{1,0:T(8,128)}), f32[32,1024]{1,0:T(8,128)}) %reduce-scatter.21.cloned.1.call-update) | async-done | bytes 131088
  918.0 151.7 %reduce-scatter.19.cloned.1.call-done = f32[32,1024]{1,0:T(8,128)} async-done(((f32[1024,1024]{1,0:T(8,128)}), f32[32,1024]{1,0:T(8,128)}) %reduce-scatter.19.cloned.1.call-update) | async-done | bytes 131088
  1069.7 362.3 %reduce-scatter.17.cloned.1.call-done = f32[128,1024]{1,0:T(8,128)} async-done(((f32[4096,1024]{1,0:T(8,128)}), f32[128,1024]{1,0:T(8,128)}) %reduce-scatter.17.cloned.1.call-update) | async-done | bytes 524304 | tf_op jit(solution)/shard_map/reduce_scatter | solution.py:231
  1432.0 364.7 %reduce-scatter.15.cloned.1.call-done = f32[32,4096]{1,0:T(8,128)} async-done(((f32[1024,4096]{1,0:T(8,128)}), f32[32,4096]{1,0:T(8,128)}) %reduce-scatter.15.cloned.1.call-update) | async-done | bytes 524304 | tf_op jit(solution)/shard_map/reduce_scatter | solution.py:231
  (710 shorter events, 403.0 us)
Async XLA Ops:
  7.2 214.1 %copy-start = (bf16[1024,1024]{1,0:T(8,128)(2,1)S(1)}, bf16[1024,1024]{1,0:T(8,128)(2,1)}, u32[]{:S(2)}) copy-start(bf16[1024,1024]{1,0:T(8,128)(2,1)} %param.26) | copy-start | bytes 6291460
  22.5 26.6 %all-to-all-start.6 = ((bf16[3,1,128,4,256]{4,2,1,0,3:T(8,128)(2,1)}), bf16[3,1,128,4,256]{4,2,1,0,3:T(8,128)(2,1)}, u32[]{:S(2)}, u32[]{:S(2)}) async-start(bf16[3,1,128,4,256]{4,2,1,0,3:T(8,128)(2,1)} %pad_maximum_fusion.9), calls=%async_computation.6 | async-start | bytes 1572864 | tf_op jit(solution)/shard_map/all_to_all | solution.py:110
  49.1 23.9 %all-to-all-start.4 = ((bf16[3,1,128,4,256]{4,2,1,0,3:T(8,128)(2,1)}), bf16[3,1,128,4,256]{4,2,1,0,3:T(8,128)(2,1)}, u32[]{:S(2)}, u32[]{:S(2)}) async-start(bf16[3,1,128,4,256]{4,2,1,0,3:T(8,128)(2,1)} %pad_maximum_fusion.8), calls=%async_computation.4 | async-start | bytes 1572864 | tf_op jit(solution)/shard_map/all_to_all | solution.py:110
  73.0 23.9 %all-to-all-start.2 = ((bf16[3,1,128,4,256]{4,2,1,0,3:T(8,128)(2,1)}), bf16[3,1,128,4,256]{4,2,1,0,3:T(8,128)(2,1)}, u32[]{:S(2)}, u32[]{:S(2)}) async-start(bf16[3,1,128,4,256]{4,2,1,0,3:T(8,128)(2,1)} %pad_maximum_fusion.7), calls=%async_computation.2 | async-start | bytes 1572864 | tf_op jit(solution)/shard_map/all_to_all | solution.py:110
  96.9 45.7 %all-to-all-start = ((bf16[3,1,128,4,256]{4,2,1,0,3:T(8,128)(2,1)}), bf16[3,1,128,4,256]{4,2,1,0,3:T(8,128)(2,1)}, u32[]{:S(2)}, u32[]{:S(2)}) async-start(bf16[3,1,128,4,256]{4,2,1,0,3:T(8,128)(2,1)} %pad_maximum_fusion.6), calls=%async_computation | async-start | bytes 1572864 | tf_op jit(solution)/shard_map/all_to_all | solution.py:110
  110.0 90.2 %copy-start.65 = (bf16[512,4,64]{0,2,1:T(8,128)(2,1)}, bf16[512,4,64]{0,2,1:T(8,128)(2,1)S(1)}, u32[]{:S(2)}) copy-start(bf16[512,4,64]{0,2,1:T(8,128)(2,1)S(1)} %reshape.1119) | copy-start | bytes 786436
  168.9 42.3 %all-to-all-start.1 = ((bf16[4,2,16384]{2,1,0:T(2,128)(2,1)}), bf16[4,2,16384]{2,1,0:T(2,128)(2,1)}, u32[]{:S(2)}, u32[]{:S(2)}) async-start(bf16[4,2,16384]{2,1,0:T(2,128)(2,1)} %reshape.1151), calls=%async_computation.1 | async-start | bytes 524288 | tf_op jit(solution)/shard_map/all_to_all | solution.py:132
  211.2 22.9 %all-to-all-start.3 = ((bf16[4,2,16384]{2,1,0:T(2,128)(2,1)}), bf16[4,2,16384]{2,1,0:T(2,128)(2,1)}, u32[]{:S(2)}, u32[]{:S(2)}) async-start(bf16[4,2,16384]{2,1,0:T(2,128)(2,1)} %reshape.1149), calls=%async_computation.3 | async-start | bytes 524288 | tf_op jit(solution)/shard_map/all_to_all | solution.py:132
  221.9 126.5 %copy-start.142 = (f32[128]{0:T(128)}, f32[128]{0:T(128)S(1)}, u32[]{:S(2)}) copy-start(f32[128]{0:T(128)S(1)} %broadcast_multiply_fusion.23) | copy-start | bytes 1540
  222.2 126.3 %copy-start.150 = (f32[128]{0:T(128)}, f32[128]{0:T(128)S(1)}, u32[]{:S(2)}) copy-start(f32[128]{0:T(128)S(1)} %add_rsqrt_fusion.7) | copy-start | bytes 1540
  234.0 23.9 %all-to-all-start.5 = ((bf16[4,2,16384]{2,1,0:T(2,128)(2,1)}), bf16[4,2,16384]{2,1,0:T(2,128)(2,1)}, u32[]{:S(2)}, u32[]{:S(2)}) async-start(bf16[4,2,16384]{2,1,0:T(2,128)(2,1)} %reshape.1147), calls=%async_computation.5 | async-start | bytes 524288 | tf_op jit(solution)/shard_map/all_to_all | solution.py:132
  244.9 111.5 %copy-start.144 = (f32[128]{0:T(128)}, f32[128]{0:T(128)S(1)}, u32[]{:S(2)}) copy-start(f32[128]{0:T(128)S(1)} %broadcast_multiply_fusion.21) | copy-start | bytes 1540
  245.1 111.3 %copy-start.152 = (f32[128]{0:T(128)}, f32[128]{0:T(128)S(1)}, u32[]{:S(2)}) copy-start(f32[128]{0:T(128)S(1)} %add_rsqrt_fusion.5) | copy-start | bytes 1540
  257.9 25.3 %all-to-all-start.7 = ((bf16[4,2,16384]{2,1,0:T(2,128)(2,1)}), bf16[4,2,16384]{2,1,0:T(2,128)(2,1)}, u32[]{:S(2)}, u32[]{:S(2)}) async-start(bf16[4,2,16384]{2,1,0:T(2,128)(2,1)} %reshape.1145), calls=%async_computation.7 | async-start | bytes 524288 | tf_op jit(solution)/shard_map/all_to_all | solution.py:132
  268.6 87.9 %copy-start.146 = (f32[128]{0:T(128)}, f32[128]{0:T(128)S(1)}, u32[]{:S(2)}) copy-start(f32[128]{0:T(128)S(1)} %broadcast_multiply_fusion.19) | copy-start | bytes 1540
  268.8 87.7 %copy-start.154 = (f32[128]{0:T(128)}, f32[128]{0:T(128)S(1)}, u32[]{:S(2)}) copy-start(f32[128]{0:T(128)S(1)} %add_rsqrt_fusion.3) | copy-start | bytes 1540
  288.6 67.8 %copy-start.13 = (f32[128,1024]{1,0:T(8,128)}, f32[128,1024]{1,0:T(8,128)S(1)}, u32[]{:S(2)}) copy-start(f32[128,1024]{1,0:T(8,128)S(1)} %get-tuple-element.229) | copy-start | bytes 1572868
  288.6 67.8 %copy-start.148 = (f32[128]{0:T(128)}, f32[128]{0:T(128)S(1)}, u32[]{:S(2)}) copy-start(f32[128]{0:T(128)S(1)} %broadcast_multiply_fusion.17) | copy-start | bytes 1540
  288.9 67.6 %copy-start.180 = (f32[128]{0:T(128)}, f32[128]{0:T(128)S(1)}, u32[]{:S(2)}) copy-start(f32[128]{0:T(128)S(1)} %add_rsqrt_fusion.1) | copy-start | bytes 1540
  305.7 36.1 %copy-start.111 = (f32[128,1024]{1,0:T(8,128)}, f32[128,1024]{1,0:T(8,128)S(1)}, u32[]{:S(2)}) copy-start(f32[128,1024]{1,0:T(8,128)S(1)} %get-tuple-element.141) | copy-start | bytes 1572868
  307.5 37.2 %copy-start.113 = (f32[128,1024]{1,0:T(8,128)}, f32[128,1024]{1,0:T(8,128)S(1)}, u32[]{:S(2)}) copy-start(f32[128,1024]{1,0:T(8,128)S(1)} %get-tuple-element.143) | copy-start | bytes 1572868
  307.5 41.0 %copy-start.39 = (f32[128,1024]{1,0:T(8,128)}, f32[128,1024]{1,0:T(8,128)S(1)}, u32[]{:S(2)}) copy-start(f32[128,1024]{1,0:T(8,128)S(1)} %get-tuple-element.157) | copy-start | bytes 1572868
  314.9 29.7 %copy-start.50 = (bf16[128,4096]{1,0:T(8,128)(2,1)}, bf16[128,4096]{1,0:T(8,128)(2,1)S(1)}, u32[]{:S(2)}) copy-start(bf16[128,4096]{1,0:T(8,128)(2,1)S(1)} %get-tuple-element.253) | copy-start | bytes 3145732
  322.5 26.0 %copy-start.48 = (bf16[128,4096]{1,0:T(8,128)(2,1)}, bf16[128,4096]{1,0:T(8,128)(2,1)S(1)}, u32[]{:S(2)}) copy-start(bf16[128,4096]{1,0:T(8,128)(2,1)S(1)} %get-tuple-element.249) | copy-start | bytes 3145732
  377.8 12.5 all-to-all-start.8
  382.9 433.3 %reduce-scatter.13.cloned.1.call-start = ((), (), s32[]{:S(2)}) async-start(), calls=%async_computation.22 | async-start | bytes 4325376 | tf_op jit(solution)/shard_map/reduce_scatter | solution.py:231
  390.4 15.6 all-to-all-start.12
  406.0 25.0 %all-to-all-start.14 = ((bf16[1,128,4,256]{3,1,0,2:T(8,128)(2,1)}), bf16[1,128,4,256]{3,1,0,2:T(8,128)(2,1)}, u32[]{:S(2)}, u32[]{:S(2)}) async-start(bf16[1,128,4,256]{3,1,0,2:T(8,128)(2,1)} %copy.244), calls=%async_computation.14 | async-start | bytes 524288 | tf_op jit(solution)/shard_map/all_to_all | solution.py:184
  431.0 17.9 all-to-all-start.10
  448.9 45.1 %all-to-all-start.9 = ((bf16[3,1,512,1,256]{4,0,3,1,2:T(4,128)(2,1)}), bf16[3,1,512,1,256]{4,0,3,1,2:T(4,128)(2,1)}, u32[]{:S(2)}, u32[]{:S(2)}) async-start(bf16[3,1,512,1,256]{4,0,3,1,2:T(4,128)(2,1)} %pad_maximum_fusion.2), calls=%async_computation.9 | async-start | bytes 2097152 | tf_op jit(solution)/shard_map/all_to_all | solution.py:213
  455.6 43.0 %copy-start.73 = (bf16[512,4,64]{0,2,1:T(8,128)(2,1)}, bf16[512,4,64]{0,2,1:T(8,128)(2,1)S(1)}, u32[]{:S(2)}) copy-start(bf16[512,4,64]{0,2,1:T(8,128)(2,1)S(1)} %reshape.1127) | copy-start | bytes 786436
  466.4 32.3 %copy-start.134 = (f32[4,512]{1,0:T(4,128)S(1)}, f32[4,512]{1,0:T(4,128)}, u32[]{:S(2)}) copy-start(f32[4,512]{1,0:T(4,128)} %log_add_fusion.2) | copy-start | bytes 24580
  494.0 44.9 %all-to-all-start.13 = ((bf16[3,1,512,1,256]{4,0,3,1,2:T(4,128)(2,1)}), bf16[3,1,512,1,256]{4,0,3,1,2:T(4,128)(2,1)}, u32[]{:S(2)}, u32[]{:S(2)}) async-start(bf16[3,1,512,1,256]{4,0,3,1,2:T(4,128)(2,1)} %pad_maximum_fusion.4), calls=%async_computation.13 | async-start | bytes 2097152 | tf_op jit(solution)/shard_map/all_to_all | solution.py:213
  538.9 36.0 %all-to-all-start.15 = ((bf16[3,1,512,1,256]{4,0,3,1,2:T(4,128)(2,1)}), bf16[3,1,512,1,256]{4,0,3,1,2:T(4,128)(2,1)}, u32[]{:S(2)}, u32[]{:S(2)}) async-start(bf16[3,1,512,1,256]{4,0,3,1,2:T(4,128)(2,1)} %pad_maximum_fusion.5), calls=%async_computation.15 | async-start | bytes 2097152 | tf_op jit(solution)/shard_map/all_to_all | solution.py:213
  574.9 29.9 %all-to-all-start.11 = ((bf16[3,1,512,1,256]{4,0,3,1,2:T(4,128)(2,1)}), bf16[3,1,512,1,256]{4,0,3,1,2:T(4,128)(2,1)}, u32[]{:S(2)}, u32[]{:S(2)}) async-start(bf16[3,1,512,1,256]{4,0,3,1,2:T(4,128)(2,1)} %pad_maximum_fusion.3), calls=%async_computation.11 | async-start | bytes 2097152 | tf_op jit(solution)/shard_map/all_to_all | solution.py:213
  579.1 237.1 %reduce-scatter.23.cloned.1.call-start = ((), (), s32[]{:S(2)}) async-start(), calls=%async_computation.27 | async-start | bytes 4325376
  581.8 27.9 %copy-start.79 = (bf16[1,1,128,4,1,256]{2,5,3,4,1,0:T(8,128)(2,1)}, bf16[1,1,128,4,1,256]{2,5,3,4,1,0:T(8,128)(2,1)S(1)}, u32[]{:S(2)}) copy-start(bf16[1,1,128,4,1,256]{2,5,3,4,1,0:T(8,128)(2,1)S(1)} %copy.219) | copy-start | bytes 786436
  584.3 24.7 %copy-start.77 = (bf16[1,1,128,4,1,256]{2,5,3,4,1,0:T(8,128)(2,1)}, bf16[1,1,128,4,1,256]{2,5,3,4,1,0:T(8,128)(2,1)S(1)}, u32[]{:S(2)}) copy-start(bf16[1,1,128,4,1,256]{2,5,3,4,1,0:T(8,128)(2,1)S(1)} %copy.243) | copy-start | bytes 786436
  585.7 21.4 %copy-start.37 = (bf16[3,1,512,1,256]{4,2,0,3,1:T(8,128)(2,1)}, bf16[3,1,512,1,256]{4,2,0,3,1:T(8,128)(2,1)S(1)}, u32[]{:S(2)}) copy-start(bf16[3,1,512,1,256]{4,2,0,3,1:T(8,128)(2,1)S(1)} %copy.252) | copy-start | bytes 2359300
  587.9 22.5 %copy-start.59 = (bf16[1,1,128,4,1,256]{2,5,3,4,1,0:T(8,128)(2,1)}, bf16[1,1,128,4,1,256]{2,5,3,4,1,0:T(8,128)(2,1)S(1)}, u32[]{:S(2)}) copy-start(bf16[1,1,128,4,1,256]{2,5,3,4,1,0:T(8,128)(2,1)S(1)} %copy.255) | copy-start | bytes 786436
  618.5 299.5 %reduce-scatter.21.cloned.1.call-start = ((), (), s32[]{:S(2)}) async-start(), calls=%async_computation.26 | async-start | bytes 4325376
  630.4 439.3 %reduce-scatter.19.cloned.1.call-start = ((), (), s32[]{:S(2)}) async-start(), calls=%async_computation.25 | async-start | bytes 4325376
  642.3 789.7 %reduce-scatter.17.cloned.1.call-start = ((), (), s32[]{:S(2)}) async-start(), calls=%async_computation.24 | async-start | bytes 17301504 | tf_op jit(solution)/shard_map/reduce_scatter | solution.py:231
  697.4 1099.2 %reduce-scatter.15.cloned.1.call-start = ((), (), s32[]{:S(2)}) async-start(), calls=%async_computation.23 | async-start | bytes 17301504 | tf_op jit(solution)/shard_map/reduce_scatter | solution.py:231
  747.8 53.6 %copy-start.2 = (bf16[1024,1024]{1,0:T(8,128)(2,1)S(1)}, bf16[1024,1024]{1,0:T(8,128)(2,1)}, u32[]{:S(2)}) copy-start(bf16[1024,1024]{1,0:T(8,128)(2,1)} %param.21) | copy-start | bytes 6291460
  747.8 53.6 %copy-start.29 = (f32[128,1024]{1,0:T(8,128)S(1)}, f32[128,1024]{1,0:T(8,128)}, u32[]{:S(2)}) copy-start(f32[128,1024]{1,0:T(8,128)} %copy-done.28) | copy-start | bytes 1572868
  754.9 48.2 %copy-start.88 = (bf16[1,1,128,4,1,256]{2,5,3,4,1,0:T(8,128)(2,1)S(1)}, bf16[1,1,128,4,1,256]{2,5,3,4,1,0:T(8,128)(2,1)}, u32[]{:S(2)}) copy-start(bf16[1,1,128,4,1,256]{2,5,3,4,1,0:T(8,128)(2,1)} %copy-done.87) | copy-start | bytes 786436
  813.8 982.8 %copy-start.1 = (bf16[1024,1024]{1,0:T(8,128)(2,1)S(1)}, bf16[1024,1024]{1,0:T(8,128)(2,1)}, u32[]{:S(2)}) copy-start(bf16[1024,1024]{1,0:T(8,128)(2,1)} %param.26) | copy-start | bytes 6291460
  (166 other events, 772.5 us)
Sparse Core Ops, SparseCore 0:
  390.5 174.6 reduce-scatter.12
  618.6 148.8 reduce-scatter.22
  770.3 147.6 reduce-scatter.20
  920.7 148.9 reduce-scatter.18
  1072.4 359.5 reduce-scatter.16
  1434.7 361.8 reduce-scatter.14
where the time goes:
time: 1820 us; the launch traced here: 1800 us
  waiting for transfers between devices  1080 us (59%)
  matrix products  324 us (18%)
  local copies, waits for them, and re-layouts  188 us (10%)
  other arithmetic  80.2 us (4%)
  starting transfers between devices  79 us (4%)
  blocking collectives  39.9 us (2%)
    reduce_scatter x3, waiting for transfers between devices, on_device(): lax.psum_scatter(lower_totals + upper_totals, ('dp', 'seq'), scatter_dime...  727 us
    unnamed x9, waiting for transfers between devices  254 us
    dot_general x24, matrix products, weight_term(): lax.dot_general(left, right, (((0,), (0,)), ((), ())), preferred_element_...  132 us
    all_to_all x4, waiting for transfers between devices, on_device(): lax.all_to_all(stacked, 'seq', split_axis=2, concat_axis=3, tiled=True)  78.3 us
    dot_general x24, matrix products, dense(): return jnp.dot(left, right, preferred_element_type=jnp.float32)  77.9 us
    dot_general x24, matrix products, dense_back(): lax.dot_general(left, right, (((1,), (1,)), ((), ())), preferred_element_...  61.9 us
    unnamed x411, local copies, waits for them, and re-layouts  53.2 us
    unnamed x1, blocking collectives  39.9 us
  transfers between devices with their start and end apart: 22, of which 13 were waited for; matrix products, arithmetic and copies ran while one was open for 25% of the time, Pallas kernels for 0%

commit v1 on v0

--- a/solution.py
+++ b/solution.py
@@ -1,12 +1,23 @@
+import functools
 import math
 import jax
 import jax.numpy as jnp
 from jax import lax
 from jax.sharding import PartitionSpec as P
+from jax.lax import all_to_all, axis_size
 
 HEAD_DIM = 64
 MICRO = 4
 EPS = 1e-05
+
+
+def handle_sources_all_over_axis(mine_x, a_name):
+    b_next = jnp.stack(jnp.split(mine_x, axis_size(a_name), 2))
+    small = all_to_all(b_next, axis_name=a_name, split_axis=0, concat_axis=0)
+    return jnp.concatenate(small, 3)
+
+
+rounds_link = functools.partial(handle_sources_all_over_axis, a_name="seq")
 
 
 def dense(left, right):
@@ -210,9 +221,7 @@
         )
         stacked = jnp.stack([d_queries, d_keys, d_vals]).astype(jnp.bfloat16)
         stacked = stacked.reshape(3, group, slots_all, 1, local_width)
-        returned = lax.all_to_all(stacked, "seq", split_axis=2, concat_axis=3, tiled=True).reshape(
-            3, rows, width
-        )
+        returned = rounds_link(stacked).reshape(3, rows, width)
         g_w_query = weight_term(block, returned[0])
         g_b_query = jnp.sum(returned[0].astype(jnp.float32), 0)
         g_w_key = weight_term(block, returned[1])

time: 1820 us -> 1770 us (0.973)
  local copies, waits for them, and re-layouts: 188 us -> 152 us
    another operation x28 -> x24, local copies, waits for them, and re-layouts: 41.2 us -> 15.7 us
  transfers between devices with their start and end apart: 22 -> 22, of which waited for: 13 -> 14; matrix products, arithmetic and copies ran while one was open for 25% -> 22% of each run, Pallas kernels for 0% -> 0%
where the time goes in v1:
time: 1770 us; the launch traced here: 1760 us
  waiting for transfers between devices  1090 us (62%)
  matrix products  316 us (18%)
  local copies, waits for them, and re-layouts  152 us (9%)
  starting transfers between devices  79.9 us (5%)
  other arithmetic  64.3 us (4%)
  blocking collectives  43.9 us (2%)
    reduce_scatter x3, waiting for transfers between devices, on_device(): lax.psum_scatter(lower_totals + upper_totals, ('dp', 'seq'), scatter_dime...  727 us
    unnamed x9, waiting for transfers between devices  254 us
    dot_general x24, matrix products, weight_term(): lax.dot_general(left, right, (((0,), (0,)), ((), ())), preferred_element_...  132 us
    all_to_all x4, waiting for transfers between devices, handle_sources_all_over_axis(): small = all_to_all(b_next, axis_name=a_name, split_axis=0, concat_axis=0)  85.1 us
    dot_general x24, matrix products, dense(): return jnp.dot(left, right, preferred_element_type=jnp.float32)  78.1 us
    dot_general x24, matrix products, dense_back(): lax.dot_general(left, right, (((1,), (1,)), ((), ())), preferred_element_...  61.7 us
    unnamed x411, local copies, waits for them, and re-layouts  54.3 us
    unnamed x1, blocking collectives  43.9 us
  transfers between devices with their start and end apart: 22, of which 14 were waited for; matrix products, arithmetic and copies ran while one was open for 22% of the time, Pallas kernels for 0%

profile of v1, /device:TPU:0, one launch (start us, length us, event | category | flops | bytes accessed | tf_op | source)
XLA Modules:
  0.0 1762.7 jit_solution(1825769466831503833)
XLA Ops:
  22.5 6.3 all-to-all-start.6
  44.0 5.1 all-to-all-done.6
  49.1 4.2 all-to-all-start.4
  68.4 4.6 all-to-all-done.4
  73.0 4.2 all-to-all-start.2
  97.0 4.4 all-to-all-start
  158.9 5.3 all-to-all-start.1
  201.3 5.5 all-to-all-start.3
  212.6 5.4 convolution_add_fusion.3
  218.0 6.3 fusion.296
  224.4 5.3 all-to-all-start.5
  235.3 5.4 convolution_add_fusion.2
  240.8 5.6 fusion.293
  248.1 5.3 all-to-all-start.7
  259.0 4.7 convolution_add_fusion.1
  263.8 9.7 fusion.302
  279.1 4.7 convolution_add_fusion
  283.9 9.4 fusion.299
  298.0 7.4 convert_reduce_fusion.3
  305.5 7.5 convert_reduce_fusion
  313.8 8.1 convert_reduce_fusion.1
  324.8 7.2 convert_reduce_fusion.2
  368.2 5.1 all-to-all-start.8
  373.3 7.4 add_add_fusion.2
  380.7 5.2 all-to-all-start.12
  423.0 5.2 all-to-all-done.14
  431.9 4.7 all-to-all-start.9
  446.1 21.8 %all-to-all-done.9 = bf16[4,3,1,128,1,256]{3,5,1,4,2,0:T(8,128)(2,1)} async-done(((bf16[4,3,1,128,1,256]{3,5,1,4,2,0:T(8,128)(2,1)}), bf16[4,3,1,128,1,256]{3,5,1,4,2,0:T(8,128)(2,1)}, u32[]{:S(2)}, u32[]{:S(2)}) %all-to-all-start.9) | async-done | bytes 786464 | tf_op jit(solution)/shard_map/all_to_all | solution.py:16
  478.2 23.6 %all-to-all-done.13 = bf16[4,3,1,128,1,256]{3,5,1,4,2,0:T(8,128)(2,1)} async-done(((bf16[4,3,1,128,1,256]{3,5,1,4,2,0:T(8,128)(2,1)}), bf16[4,3,1,128,1,256]{3,5,1,4,2,0:T(8,128)(2,1)}, u32[]{:S(2)}, u32[]{:S(2)}) %all-to-all-start.13) | async-done | bytes 786464 | tf_op jit(solution)/shard_map/all_to_all | solution.py:16
  501.8 7.7 all-to-all-start.15
  514.7 26.8 %all-to-all-done.15 = bf16[4,3,1,128,1,256]{3,5,1,4,2,0:T(8,128)(2,1)} async-done(((bf16[4,3,1,128,1,256]{3,5,1,4,2,0:T(8,128)(2,1)}), bf16[4,3,1,128,1,256]{3,5,1,4,2,0:T(8,128)(2,1)}, u32[]{:S(2)}, u32[]{:S(2)}) %all-to-all-start.15) | async-done | bytes 786464 | tf_op jit(solution)/shard_map/all_to_all | solution.py:16
  550.5 13.0 all-to-all-done.11
  569.0 5.4 copy.275
  580.0 5.4 copy.273
  590.8 5.4 copy.271
  597.9 9.7 fusion.252
  607.6 9.8 fusion.246
  617.4 9.7 fusion.240
  627.1 24.0 %add_add_fusion = f32[4096,1024]{1,0:T(8,128)} fusion(f32[4096,1024]{1,0:T(8,128)} %fusion.240, f32[4096,1024]{1,0:T(8,128)} %fusion.252, f32[4096,1024]{1,0:T(8,128)} %fusion.246, f32[128,1024]{1,0:T(8,128)S(1)} %copy-done.38, f32[128,4096]{1,0:T(8,128)S(1)} %copy-done.26), kind=kOutput, calls=%fused_computation | convolution fusion | flops 1120534528 | bytes 69730304 | tf_op jit(solution)/shard_map/dot_general | solution.py:34
  652.2 9.4 fusion.257
  661.7 8.2 fusion.260
  669.9 8.2 fusion.263
  678.1 23.2 %add_add_fusion.1 = f32[1024,4096]{1,0:T(8,128)} fusion(f32[1024,4096]{1,0:T(8,128)} %fusion.257, f32[1024,4096]{1,0:T(8,128)} %fusion.263, f32[1024,4096]{1,0:T(8,128)} %fusion.260, bf16[128,4096]{1,0:T(8,128)(2,1)S(1)} %copy-done.47, f32[128,1024]{1,0:T(8,128)S(1)} %copy-done.15, f32[128]{0:T(128)S(1)} %copy-done.181, f32[128]{0:T(128)S(1)} %copy-done.149, ...), kind=kOutput, calls=%fused_computation.1 | convolution fusion | flops 1086980096 | bytes 68690944 | tf_op jit(solution)/shard_map/dot_general | solution.py:34
  710.5 43.9 %all-reduce.9 = (f32[1024]{0:T(1024)S(1)}, f32[1024]{0:T(1024)S(1)}, f32[1024]{0:T(1024)S(1)}, f32[1024]{0:T(1024)S(1)}, f32[1024]{0:T(1024)S(1)}, /*index=5*/f3...) all-reduce(f32[1024]{0:T(1024)S(1)} %bitcast.541, ...), channel_id=3, replica_groups=mesh['dp'=8,'seq'=4] {'dp','seq'}, use_global_device_ids=true, to_apply=%region_49.50.clone | all-reduce | flops 12288 | bytes 98304
  774.5 103.2 %reduce-scatter.21.cloned.1.call-done = f32[32,1024]{1,0:T(8,128)} async-done(((f32[1024,1024]{1,0:T(8,128)}), f32[32,1024]{1,0:T(8,128)}) %reduce-scatter.21.cloned.1.call-update) | async-done | bytes 131088
  877.7 150.5 %reduce-scatter.19.cloned.1.call-done = f32[32,1024]{1,0:T(8,128)} async-done(((f32[1024,1024]{1,0:T(8,128)}), f32[32,1024]{1,0:T(8,128)}) %reduce-scatter.19.cloned.1.call-update) | async-done | bytes 131088
  1028.2 362.5 %reduce-scatter.17.cloned.1.call-done = f32[128,1024]{1,0:T(8,128)} async-done(((f32[4096,1024]{1,0:T(8,128)}), f32[128,1024]{1,0:T(8,128)}) %reduce-scatter.17.cloned.1.call-update) | async-done | bytes 524304 | tf_op jit(solution)/shard_map/reduce_scatter | solution.py:240
  1390.7 364.7 %reduce-scatter.15.cloned.1.call-done = f32[32,4096]{1,0:T(8,128)} async-done(((f32[1024,4096]{1,0:T(8,128)}), f32[32,4096]{1,0:T(8,128)}) %reduce-scatter.15.cloned.1.call-update) | async-done | bytes 524304 | tf_op jit(solution)/shard_map/reduce_scatter | solution.py:240
  (694 shorter events, 349.8 us)
Async XLA Ops:
  7.2 204.5 %copy-start = (bf16[1024,1024]{1,0:T(8,128)(2,1)S(1)}, bf16[1024,1024]{1,0:T(8,128)(2,1)}, u32[]{:S(2)}) copy-start(bf16[1024,1024]{1,0:T(8,128)(2,1)} %param.26) | copy-start | bytes 6291460
  22.5 26.6 %all-to-all-start.6 = ((bf16[3,1,128,4,256]{4,2,1,0,3:T(8,128)(2,1)}), bf16[3,1,128,4,256]{4,2,1,0,3:T(8,128)(2,1)}, u32[]{:S(2)}, u32[]{:S(2)}) async-start(bf16[3,1,128,4,256]{4,2,1,0,3:T(8,128)(2,1)} %pad_maximum_fusion.5), calls=%async_computation.6 | async-start | bytes 1572864 | tf_op jit(solution)/shard_map/all_to_all | solution.py:121
  49.1 24.0 %all-to-all-start.4 = ((bf16[3,1,128,4,256]{4,2,1,0,3:T(8,128)(2,1)}), bf16[3,1,128,4,256]{4,2,1,0,3:T(8,128)(2,1)}, u32[]{:S(2)}, u32[]{:S(2)}) async-start(bf16[3,1,128,4,256]{4,2,1,0,3:T(8,128)(2,1)} %pad_maximum_fusion.4), calls=%async_computation.4 | async-start | bytes 1572864 | tf_op jit(solution)/shard_map/all_to_all | solution.py:121
  73.0 23.9 %all-to-all-start.2 = ((bf16[3,1,128,4,256]{4,2,1,0,3:T(8,128)(2,1)}), bf16[3,1,128,4,256]{4,2,1,0,3:T(8,128)(2,1)}, u32[]{:S(2)}, u32[]{:S(2)}) async-start(bf16[3,1,128,4,256]{4,2,1,0,3:T(8,128)(2,1)} %pad_maximum_fusion.3), calls=%async_computation.2 | async-start | bytes 1572864 | tf_op jit(solution)/shard_map/all_to_all | solution.py:121
  97.0 35.7 %all-to-all-start = ((bf16[3,1,128,4,256]{4,2,1,0,3:T(8,128)(2,1)}), bf16[3,1,128,4,256]{4,2,1,0,3:T(8,128)(2,1)}, u32[]{:S(2)}, u32[]{:S(2)}) async-start(bf16[3,1,128,4,256]{4,2,1,0,3:T(8,128)(2,1)} %pad_maximum_fusion.2), calls=%async_computation | async-start | bytes 1572864 | tf_op jit(solution)/shard_map/all_to_all | solution.py:121
  125.4 38.9 %copy-start.63 = (bf16[512,4,64]{0,2,1:T(8,128)(2,1)}, bf16[512,4,64]{0,2,1:T(8,128)(2,1)S(1)}, u32[]{:S(2)}) copy-start(bf16[512,4,64]{0,2,1:T(8,128)(2,1)S(1)} %reshape.1109) | copy-start | bytes 786436
  158.9 42.4 %all-to-all-start.1 = ((bf16[4,2,16384]{2,1,0:T(2,128)(2,1)}), bf16[4,2,16384]{2,1,0:T(2,128)(2,1)}, u32[]{:S(2)}, u32[]{:S(2)}) async-start(bf16[4,2,16384]{2,1,0:T(2,128)(2,1)} %reshape.1159), calls=%async_computation.1 | async-start | bytes 524288 | tf_op jit(solution)/shard_map/all_to_all | solution.py:143
  201.3 23.1 %all-to-all-start.3 = ((bf16[4,2,16384]{2,1,0:T(2,128)(2,1)}), bf16[4,2,16384]{2,1,0:T(2,128)(2,1)}, u32[]{:S(2)}, u32[]{:S(2)}) async-start(bf16[4,2,16384]{2,1,0:T(2,128)(2,1)} %reshape.1157), calls=%async_computation.3 | async-start | bytes 524288 | tf_op jit(solution)/shard_map/all_to_all | solution.py:143
  212.3 126.4 %copy-start.142 = (f32[128]{0:T(128)}, f32[128]{0:T(128)S(1)}, u32[]{:S(2)}) copy-start(f32[128]{0:T(128)S(1)} %broadcast_multiply_fusion.23) | copy-start | bytes 1540
  212.5 126.2 %copy-start.150 = (f32[128]{0:T(128)}, f32[128]{0:T(128)S(1)}, u32[]{:S(2)}) copy-start(f32[128]{0:T(128)S(1)} %add_rsqrt_fusion.7) | copy-start | bytes 1540
  224.4 23.7 %all-to-all-start.5 = ((bf16[4,2,16384]{2,1,0:T(2,128)(2,1)}), bf16[4,2,16384]{2,1,0:T(2,128)(2,1)}, u32[]{:S(2)}, u32[]{:S(2)}) async-start(bf16[4,2,16384]{2,1,0:T(2,128)(2,1)} %reshape.1155), calls=%async_computation.5 | async-start | bytes 524288 | tf_op jit(solution)/shard_map/all_to_all | solution.py:143
  235.1 111.6 %copy-start.144 = (f32[128]{0:T(128)}, f32[128]{0:T(128)S(1)}, u32[]{:S(2)}) copy-start(f32[128]{0:T(128)S(1)} %broadcast_multiply_fusion.21) | copy-start | bytes 1540
  235.3 111.4 %copy-start.152 = (f32[128]{0:T(128)}, f32[128]{0:T(128)S(1)}, u32[]{:S(2)}) copy-start(f32[128]{0:T(128)S(1)} %add_rsqrt_fusion.5) | copy-start | bytes 1540
  248.1 25.4 %all-to-all-start.7 = ((bf16[4,2,16384]{2,1,0:T(2,128)(2,1)}), bf16[4,2,16384]{2,1,0:T(2,128)(2,1)}, u32[]{:S(2)}, u32[]{:S(2)}) async-start(bf16[4,2,16384]{2,1,0:T(2,128)(2,1)} %reshape.1153), calls=%async_computation.7 | async-start | bytes 524288 | tf_op jit(solution)/shard_map/all_to_all | solution.py:143
  258.8 87.9 %copy-start.146 = (f32[128]{0:T(128)}, f32[128]{0:T(128)S(1)}, u32[]{:S(2)}) copy-start(f32[128]{0:T(128)S(1)} %broadcast_multiply_fusion.19) | copy-start | bytes 1540
  259.0 87.7 %copy-start.154 = (f32[128]{0:T(128)}, f32[128]{0:T(128)S(1)}, u32[]{:S(2)}) copy-start(f32[128]{0:T(128)S(1)} %add_rsqrt_fusion.3) | copy-start | bytes 1540
  278.8 67.9 %copy-start.14 = (f32[128,1024]{1,0:T(8,128)}, f32[128,1024]{1,0:T(8,128)S(1)}, u32[]{:S(2)}) copy-start(f32[128,1024]{1,0:T(8,128)S(1)} %get-tuple-element.249) | copy-start | bytes 1572868
  278.9 67.9 %copy-start.148 = (f32[128]{0:T(128)}, f32[128]{0:T(128)S(1)}, u32[]{:S(2)}) copy-start(f32[128]{0:T(128)S(1)} %broadcast_multiply_fusion.17) | copy-start | bytes 1540
  279.1 67.7 %copy-start.180 = (f32[128]{0:T(128)}, f32[128]{0:T(128)S(1)}, u32[]{:S(2)}) copy-start(f32[128]{0:T(128)S(1)} %add_rsqrt_fusion.1) | copy-start | bytes 1540
  296.1 35.9 %copy-start.115 = (f32[128,1024]{1,0:T(8,128)}, f32[128,1024]{1,0:T(8,128)S(1)}, u32[]{:S(2)}) copy-start(f32[128,1024]{1,0:T(8,128)S(1)} %get-tuple-element.141) | copy-start | bytes 1572868
  298.0 37.0 %copy-start.117 = (f32[128,1024]{1,0:T(8,128)}, f32[128,1024]{1,0:T(8,128)S(1)}, u32[]{:S(2)}) copy-start(f32[128,1024]{1,0:T(8,128)S(1)} %get-tuple-element.143) | copy-start | bytes 1572868
  298.0 40.7 %copy-start.37 = (f32[128,1024]{1,0:T(8,128)}, f32[128,1024]{1,0:T(8,128)S(1)}, u32[]{:S(2)}) copy-start(f32[128,1024]{1,0:T(8,128)S(1)} %get-tuple-element.157) | copy-start | bytes 1572868
  305.4 29.5 %copy-start.48 = (bf16[128,4096]{1,0:T(8,128)(2,1)}, bf16[128,4096]{1,0:T(8,128)(2,1)S(1)}, u32[]{:S(2)}) copy-start(bf16[128,4096]{1,0:T(8,128)(2,1)S(1)} %get-tuple-element.273) | copy-start | bytes 3145732
  313.0 25.7 %copy-start.46 = (bf16[128,4096]{1,0:T(8,128)(2,1)}, bf16[128,4096]{1,0:T(8,128)(2,1)S(1)}, u32[]{:S(2)}) copy-start(bf16[128,4096]{1,0:T(8,128)(2,1)S(1)} %get-tuple-element.269) | copy-start | bytes 3145732
  368.2 12.5 all-to-all-start.8
  373.3 401.3 %reduce-scatter.13.cloned.1.call-start = ((), (), s32[]{:S(2)}) async-start(), calls=%async_computation.22 | async-start | bytes 4325376 | tf_op jit(solution)/shard_map/reduce_scatter | solution.py:240
  380.7 15.5 all-to-all-start.12
  396.2 16.4 all-to-all-start.10
  412.6 15.6 all-to-all-start.14
  419.1 52.9 %copy-start.74 = (bf16[512,4,64]{0,2,1:T(8,128)(2,1)}, bf16[512,4,64]{0,2,1:T(8,128)(2,1)S(1)}, u32[]{:S(2)}) copy-start(bf16[512,4,64]{0,2,1:T(8,128)(2,1)S(1)} %reshape.1132) | copy-start | bytes 786436
  431.9 36.0 %all-to-all-start.9 = ((bf16[4,3,1,128,1,256]{3,5,1,4,2,0:T(8,128)(2,1)}), bf16[4,3,1,128,1,256]{3,5,1,4,2,0:T(8,128)(2,1)}, u32[]{:S(2)}, u32[]{:S(2)}) async-start(bf16[4,3,1,128,1,256]{3,5,1,4,2,0:T(8,128)(2,1)} %pad_maximum_fusion.7), calls=%async_computation.9 | async-start | bytes 1572864 | tf_op jit(solution)/shard_map/all_to_all | solution.py:16
  444.9 27.1 %copy-start.125 = (bf16[512,4,64]{0,2,1:T(8,128)(2,1)S(1)}, bf16[512,4,64]{0,2,1:T(8,128)(2,1)}, u32[]{:S(2)}) copy-start(bf16[512,4,64]{0,2,1:T(8,128)(2,1)} %reshape.1107) | copy-start | bytes 786436
  444.9 27.1 %copy-start.134 = (f32[4,512]{1,0:T(4,128)S(1)}, f32[4,512]{1,0:T(4,128)}, u32[]{:S(2)}) copy-start(f32[4,512]{1,0:T(4,128)} %log_add_fusion.2) | copy-start | bytes 24580
  467.8 34.0 %all-to-all-start.13 = ((bf16[4,3,1,128,1,256]{3,5,1,4,2,0:T(8,128)(2,1)}), bf16[4,3,1,128,1,256]{3,5,1,4,2,0:T(8,128)(2,1)}, u32[]{:S(2)}, u32[]{:S(2)}) async-start(bf16[4,3,1,128,1,256]{3,5,1,4,2,0:T(8,128)(2,1)} %pad_maximum_fusion.11), calls=%async_computation.13 | async-start | bytes 1572864 | tf_op jit(solution)/shard_map/all_to_all | solution.py:16
  476.8 32.7 %copy-start.64 = (bf16[512,4,64]{0,2,1:T(8,128)(2,1)S(1)}, bf16[512,4,64]{0,2,1:T(8,128)(2,1)}, u32[]{:S(2)}) copy-start(bf16[512,4,64]{0,2,1:T(8,128)(2,1)} %copy-done.63) | copy-start | bytes 786436
  501.8 39.7 %all-to-all-start.15 = ((bf16[4,3,1,128,1,256]{3,5,1,4,2,0:T(8,128)(2,1)}), bf16[4,3,1,128,1,256]{3,5,1,4,2,0:T(8,128)(2,1)}, u32[]{:S(2)}, u32[]{:S(2)}) async-start(bf16[4,3,1,128,1,256]{3,5,1,4,2,0:T(8,128)(2,1)} %pad_maximum_fusion.13), calls=%async_computation.15 | async-start | bytes 1572864 | tf_op jit(solution)/shard_map/all_to_all | solution.py:16
  541.5 21.9 %all-to-all-start.11 = ((bf16[4,3,1,128,1,256]{3,5,1,4,2,0:T(8,128)(2,1)}), bf16[4,3,1,128,1,256]{3,5,1,4,2,0:T(8,128)(2,1)S(1)}, u32[]{:S(2)}, u32[]{:S(2)}) async-start(bf16[4,3,1,128,1,256]{3,5,1,4,2,0:T(8,128)(2,1)} %pad_maximum_fusion.9), calls=%async_computation.11 | async-start | bytes 1572864 | tf_op jit(solution)/shard_map/all_to_all | solution.py:16
  545.2 229.3 %reduce-scatter.23.cloned.1.call-start = ((), (), s32[]{:S(2)}) async-start(), calls=%async_computation.27 | async-start | bytes 4325376
  550.5 26.8 %copy-start.59 = (bf16[1,1,128,4,1,256]{2,5,0,4,1,3:T(8,128)(2,1)}, bf16[1,1,128,4,1,256]{2,5,0,4,1,3:T(8,128)(2,1)S(1)}, u32[]{:S(2)}) copy-start(bf16[1,1,128,4,1,256]{2,5,0,4,1,3:T(8,128)(2,1)S(1)} %get-tuple-element.191) | copy-start | bytes 786436
  550.5 37.6 %copy-start.61 = (bf16[1,1,128,4,1,256]{2,5,0,4,1,3:T(8,128)(2,1)}, bf16[1,1,128,4,1,256]{2,5,0,4,1,3:T(8,128)(2,1)S(1)}, u32[]{:S(2)}) copy-start(bf16[1,1,128,4,1,256]{2,5,0,4,1,3:T(8,128)(2,1)S(1)} %get-tuple-element.192) | copy-start | bytes 786436
  574.4 303.3 %reduce-scatter.21.cloned.1.call-start = ((), (), s32[]{:S(2)}) async-start(), calls=%async_computation.26 | async-start | bytes 4325376
  585.4 442.8 %reduce-scatter.19.cloned.1.call-start = ((), (), s32[]{:S(2)}) async-start(), calls=%async_computation.25 | async-start | bytes 4325376
  596.2 794.5 %reduce-scatter.17.cloned.1.call-start = ((), (), s32[]{:S(2)}) async-start(), calls=%async_computation.24 | async-start | bytes 17301504 | tf_op jit(solution)/shard_map/reduce_scatter | solution.py:240
  651.3 1104.2 %reduce-scatter.15.cloned.1.call-start = ((), (), s32[]{:S(2)}) async-start(), calls=%async_computation.23 | async-start | bytes 17301504 | tf_op jit(solution)/shard_map/reduce_scatter | solution.py:240
  701.6 58.0 %copy-start.2 = (bf16[1024,1024]{1,0:T(8,128)(2,1)S(1)}, bf16[1024,1024]{1,0:T(8,128)(2,1)}, u32[]{:S(2)}) copy-start(bf16[1024,1024]{1,0:T(8,128)(2,1)} %param.21) | copy-start | bytes 6291460
  701.7 58.0 %copy-start.30 = (f32[128,1024]{1,0:T(8,128)S(1)}, f32[128,1024]{1,0:T(8,128)}, u32[]{:S(2)}) copy-start(f32[128,1024]{1,0:T(8,128)} %copy-done.29) | copy-start | bytes 1572868
  710.4 51.0 %copy-start.102 = (bf16[1,1,128,4,1,256]{2,5,0,4,1,3:T(8,128)(2,1)S(1)}, bf16[1,1,128,4,1,256]{2,5,0,4,1,3:T(8,128)(2,1)}, u32[]{:S(2)}) copy-start(bf16[1,1,128,4,1,256]{2,5,0,4,1,3:T(8,128)(2,1)} %get-tuple-element.167) | copy-start | bytes 786436
  772.1 983.4 %copy-start.1 = (bf16[1024,1024]{1,0:T(8,128)(2,1)S(1)}, bf16[1024,1024]{1,0:T(8,128)(2,1)}, u32[]{:S(2)}) copy-start(bf16[1024,1024]{1,0:T(8,128)(2,1)} %param.26) | copy-start | bytes 6291460
  (166 other events, 837.0 us)
Sparse Core Ops, SparseCore 0:
  380.8 168.8 reduce-scatter.12
  574.5 151.9 reduce-scatter.22
  729.4 148.3 reduce-scatter.20
  880.4 147.7 reduce-scatter.18
  1030.9 359.7 reduce-scatter.16
  1393.5 361.9 reduce-scatter.14
